TPU v7x, 512 devices: a whole 4x8x8 slice. The times are simulated.
512 devices in a mesh: member: 64 (over z, y), space: 8 (over x, core).
Axes of the slice: x: 4, y: 8, z: 8, core: 2. Of those that a mesh axis runs over, the one named last changes fastest.
Arguments:
- prior_field: bfloat16 [64, 4096, 8, 128], P('member', 'space'), may hold values from -6 to 6
- replica_predicted_readings: float32 [64, 4096, 128], P('member', 'space'), may hold values from -6 to 6
- replica_reading_noise: float32 [64, 4096, 128], P('member', 'space'), may hold values from -12 to 12
- sensor_readings: float32 [4096, 128], P('space'), may hold values from -6 to 6
- reading_noise_power: float32 [4096, 128], P('space'), may hold values from 2 to 8
- sensor_patch_tally: int32 [4096], P('space'), may hold values from 1 to 128
- sensor_patch_start: int32 [4096], replicated, may hold values from 0 to 63, as said below
- neighbour_listing: int32 [4096, 8], P('space'), may hold values from 0 to 4095, as said below
Outputs:
- increment: bfloat16 [64, 4096, 8, 128], P('member', 'space')
Inputs may be any that keep to these rules, and one draw needn't show every extreme that they name: `neighbour_listing`: every row lists 8 different observation blocks, each in a tile whose two tile indices differ from those of the state block's tile by at most one. `sensor_patch_start`: the coordinate of an observation block in tile (p, q) lies from p * 8 to p * 8 + 7.
All inputs are finite; a program needn't handle non-finite values.
Results may differ from a plain program's by a relative error of at most 0.001.
Values may be sent and summed in bfloat16 or wider, within the bound.
A program may use at most 64 MiB of HBM per device.

v0:
```python
import jax
import jax.numpy as jnp
from jax import lax
from jax.sharding import PartitionSpec as P

PATCH_CAPACITY = 128
PATCHES_PER_AREA = 8
OB_DEV = 8


def padded_2(cells, sides, width):
    for axis, dim in sides:
        count = lax.axis_size(axis)
        ends = count - 1
        head = lax.slice_in_dim(cells, 0, width, axis=dim)
        tail = lax.slice_in_dim(cells, cells.shape[dim] - width, cells.shape[dim], axis=dim)
        cells = jnp.concatenate(
            [
                lax.ppermute(tail, axis, [(i, (i + 1) % count) for i in range(ends)]),
                cells,
                lax.ppermute(head, axis, [((i + 1) % count, i) for i in range(ends)]),
            ],
            axis=dim,
        )
    return cells


def increments(depth_layers, mixing):
    numeric_items = depth_layers.astype(jnp.float32)
    anomaly = numeric_items - jnp.mean(numeric_items, axis=0, keepdims=True)
    return jnp.einsum("mslc,smn->nslc", anomaly, mixing, precision=lax.Precision.HIGHEST).astype(
        jnp.bfloat16
    )


def local(
    prior_field,
    replica_predicted_readings,
    replica_reading_noise,
    sensor_readings,
    reading_noise_power,
    sensor_patch_tally,
    sensor_patch_start,
    neighbour_listing,
):
    replica_fields = lax.axis_size("member")
    member_index = lax.axis_index("member")
    space_index = lax.axis_index("space")
    highest = lax.Precision.HIGHEST
    residual_mismatch = sensor_readings[None] + replica_reading_noise - replica_predicted_readings
    model_all, innov_all = (
        lax.all_to_all(
            replica_predicted_readings, "member", split_axis=1, concat_axis=0, tiled=True
        ),
        lax.all_to_all(residual_mismatch, "member", split_axis=1, concat_axis=0, tiled=True),
    )
    error_local = lax.dynamic_slice_in_dim(reading_noise_power, member_index * OB_DEV, OB_DEV, 0)
    count_local = lax.dynamic_slice_in_dim(sensor_patch_tally, member_index * OB_DEV, OB_DEV, 0)
    prior_deviation = model_all - jnp.mean(model_all, axis=0, keepdims=True)
    dispersion = jnp.sum(prior_deviation * prior_deviation, axis=0) / (replica_fields - 1)
    slots = jnp.arange(PATCH_CAPACITY, dtype=jnp.int32)
    active_mask = (slots[None, :] < count_local[:, None]).astype(jnp.float32)
    gain_factors = active_mask[None] * innov_all / (dispersion + error_local)[None]
    products = jnp.einsum("mbj,nbj->bmn", prior_deviation, gain_factors, precision=highest)
    padded = padded_2(
        products.reshape(1, 1, OB_DEV, replica_fields * replica_fields),
        (("member", 0), ("space", 1)),
        1,
    )
    stacked = padded.reshape(9 * OB_DEV, replica_fields * replica_fields)
    listed = lax.dynamic_slice_in_dim(
        neighbour_listing, member_index * PATCHES_PER_AREA, PATCHES_PER_AREA, 0
    )
    state_x = space_index * PATCHES_PER_AREA + jnp.arange(PATCHES_PER_AREA, dtype=jnp.int32)
    target_tile = listed // (OB_DEV * replica_fields)
    target_y = listed // OB_DEV % replica_fields
    target_x = jnp.take(sensor_patch_start, listed)
    delta_x = (state_x[:, None] - target_x).astype(jnp.float32)
    delta_y = (member_index - target_y).astype(jnp.float32)
    distance = delta_x * delta_x + delta_y * delta_y
    taper = 1.0 / (1.0 + distance / float(PATCHES_PER_AREA * PATCHES_PER_AREA))
    position = (
        (target_y - member_index + 1) * 3 + (target_tile - space_index + 1)
    ) * OB_DEV + listed % OB_DEV
    columns = jnp.arange(9 * OB_DEV, dtype=jnp.int32)
    selector = jnp.sum(
        taper[:, :, None] * (position[:, :, None] == columns[None, None, :]).astype(jnp.float32),
        axis=1,
    )
    mixing = (jnp.dot(selector, stacked, precision=highest) / (replica_fields - 1)).reshape(
        PATCHES_PER_AREA, replica_fields, replica_fields
    )
    gathered_lines = lax.all_to_all(prior_field, "member", split_axis=1, concat_axis=0, tiled=True)
    result = lax.all_to_all(
        increments(gathered_lines, mixing), "member", split_axis=0, concat_axis=1, tiled=True
    )
    return result


def solution(mesh):
    placed = (
        P("member", "space", None, None),
        P("member", "space", None),
        P("member", "space", None),
        P("space", None),
        P("space", None),
        P("space"),
        P(),
        P("space", None),
    )
    return jax.shard_map(
        local,
        mesh=mesh,
        in_specs=placed,
        out_specs=P("member", "space", None, None),
        check_vma=False,
    )
```

profile of v0, /device:TPU:3, one launch (start us, length us, event | category | flops | bytes accessed | tf_op | source)
XLA Modules:
  0.0 139.1 jit_solution(7212570018021721025)
XLA Ops:
  0.0 0.0 copy-start
  0.0 16.4 %all-to-all-start = ((f32[1,512,128]{2,0,1:T(1,128)}), f32[1,512,128]{2,0,1:T(1,128)S(1)}, u32[]{:S(2)}, u32[]{:S(2)}) async-start(f32[1,512,128]{2,0,1:T(1,128)} %bitcast.29), calls=%async_computation | async-start | bytes 524288 | tf_op jit(solution)/shard_map/all_to_all | solution.py:52
  16.5 0.0 copy-done
  16.5 0.1 constant_dynamic-slice_fusion
  16.5 0.8 dynamic_slice.10
  17.3 0.1 copy.52
  17.4 0.1 fusion.22
  17.4 1.8 %fusion.5 = f32[1,512,128]{2,1,0:T(8,128)} fusion(f32[1,512,128]{2,1,0:T(8,128)} %param.9, f32[1,512,128]{2,1,0:T(8,128)} %param.10, f32[512,128]{1,0:T(8,128)} %param.11), kind=kLoop, calls=%fused_computation.11 | loop fusion | flops 131072 | bytes 1048576 | tf_op jit(solution)/shard_map/sub | solution.py:50
  19.3 10.0 %all-to-all-done = f32[1,512,128]{2,0,1:T(1,128)S(1)} async-done(((f32[1,512,128]{2,0,1:T(1,128)}), f32[1,512,128]{2,0,1:T(1,128)S(1)}, u32[]{:S(2)}, u32[]{:S(2)}) %all-to-all-start) | async-done | bytes 262176 | tf_op jit(solution)/shard_map/all_to_all | solution.py:52
  29.3 5.7 %all-to-all-start.1 = ((f32[1,512,128]{2,0,1:T(1,128)}), f32[1,512,128]{2,0,1:T(1,128)S(1)}, u32[]{:S(2)}, u32[]{:S(2)}) async-start(f32[1,512,128]{2,0,1:T(1,128)} %bitcast.3), calls=%async_computation.1 | async-start | bytes 524288 | tf_op jit(solution)/shard_map/all_to_all | solution.py:55
  35.0 0.1 reduce_sum.37
  35.0 0.1 multiply_reduce_fusion
  35.1 0.7 dynamic-slice_add_fusion
  35.8 11.7 %all-to-all-done.1 = f32[1,512,128]{2,0,1:T(1,128)S(1)} async-done(((f32[1,512,128]{2,0,1:T(1,128)}), f32[1,512,128]{2,0,1:T(1,128)S(1)}, u32[]{:S(2)}, u32[]{:S(2)}) %all-to-all-start.1) | async-done | bytes 262176 | tf_op jit(solution)/shard_map/all_to_all | solution.py:55
  47.5 0.0 copy-start.1
  47.5 5.0 %all-to-all-start.2 = ((bf16[1,512,8,128]{3,2,0,1:T(8,128)(2,1)}), bf16[1,512,8,128]{3,2,0,1:T(8,128)(2,1)S(1)}, u32[]{:S(2)}, u32[]{:S(2)}) async-start(bf16[1,512,8,128]{3,2,0,1:T(8,128)(2,1)} %bitcast.7), calls=%async_computation.2 | async-start | bytes 2097152 | tf_op jit(solution)/shard_map/all_to_all | solution.py:93
  52.5 0.6 fusion.7
  53.1 0.1 reshape.66
  53.2 2.9 %collective-permute-start = (f32[1,1,8,4096]{3,2,1,0:T(8,128)S(1)}, f32[1,1,8,4096]{3,2,1,0:T(8,128)S(1)}, u32[]{:S(2)}, u32[]{:S(2)}) collective-permute-start(f32[1,1,8,4096]{3,2,1,0:T(8,128)S(1)} %reshape.66), channel_id=1, source_target_pairs={{0,8},{8,16},{16,24},{24,32},{32,40},{40,48},{48,56},{56,64},{64,7... | collective-permute-start | bytes 393224 | tf_op jit(solution)/shard_map/ppermute | solution.py:19
  56.2 0.1 reshape.72
  56.2 1.3 collective-permute-start.1
  57.5 15.9 %collective-permute-done = f32[1,1,8,4096]{3,2,1,0:T(8,128)S(1)} collective-permute-done((f32[1,1,8,4096]{3,2,1,0:T(8,128)S(1)}, f32[1,1,8,4096]{3,2,1,0:T(8,128)S(1)}, u32[]{:S(2)}, u32[]{:S(2)}) %collective-permute-start) | collective-permute-done | bytes 131104 | tf_op jit(solution)/shard_map/ppermute | solution.py:19
  73.4 4.1 %collective-permute-done.1 = f32[1,1,8,4096]{3,2,1,0:T(8,128)S(1)} collective-permute-done((f32[1,1,8,4096]{3,2,1,0:T(8,128)S(1)}, f32[1,1,8,4096]{3,2,1,0:T(8,128)S(1)}, u32[]{:S(2)}, u32[]{:S(2)}) %collective-permute-start.1) | collective-permute-done | bytes 131104 | tf_op jit(solution)/shard_map/ppermute | solution.py:21
  77.6 5.7 %collective-permute-start.2 = (f32[3,1,8,4096]{3,2,1,0:T(8,128)S(1)}, f32[3,1,8,4096]{3,2,1,0:T(8,128)S(1)}, u32[]{:S(2)}, u32[]{:S(2)}) collective-permute-start(f32[3,1,8,4096]{3,2,1,0:T(8,128)S(1)} %constant_dynamic-update-slice_fusion), channel_id=1, source_target_pairs={{0,1},{1,2},{2,3},{3,4},{4,5},{5,6},{6,7},{8,9},{9,10},{10,11},{11... | collective-permute-start | bytes 1179656 | tf_op jit(solution)/shard_map/ppermute | solution.py:19
  83.3 1.9 %collective-permute-start.3 = (f32[3,1,8,4096]{3,2,1,0:T(8,128)S(1)}, f32[3,1,8,4096]{3,2,1,0:T(8,128)S(1)}, u32[]{:S(2)}, u32[]{:S(2)}) collective-permute-start(f32[3,1,8,4096]{3,2,1,0:T(8,128)S(1)} %constant_dynamic-update-slice_fusion), channel_id=1, source_target_pairs={{1,0},{2,1},{3,2},{4,3},{5,4},{6,5},{7,6},{9,8},{10,9},{11,10},{12... | collective-permute-start | bytes 1179656 | tf_op jit(solution)/shard_map/ppermute | solution.py:21
  85.2 0.0 copy-done.1
  85.2 0.8 gather_fusion
  86.0 0.1 reshape.71
  86.1 0.1 add_divide_fusion
  86.2 0.1 select_reduce_fusion
  86.3 1.7 %collective-permute-done.2 = f32[3,1,8,4096]{3,2,1,0:T(8,128)S(1)} collective-permute-done((f32[3,1,8,4096]{3,2,1,0:T(8,128)S(1)}, f32[3,1,8,4096]{3,2,1,0:T(8,128)S(1)}, u32[]{:S(2)}, u32[]{:S(2)}) %collective-permute-start.2) | collective-permute-done | bytes 393248 | tf_op jit(solution)/shard_map/ppermute | solution.py:19
  88.0 4.4 %collective-permute-done.3 = f32[3,1,8,4096]{3,2,1,0:T(8,128)S(1)} collective-permute-done((f32[3,1,8,4096]{3,2,1,0:T(8,128)S(1)}, f32[3,1,8,4096]{3,2,1,0:T(8,128)S(1)}, u32[]{:S(2)}, u32[]{:S(2)}) %collective-permute-start.3) | collective-permute-done | bytes 393248 | tf_op jit(solution)/shard_map/ppermute | solution.py:21
  92.4 0.1 pad_maximum_fusion
  92.5 0.7 convolution_multiply_fusion
  93.2 0.1 reshape.68
  93.3 0.0 all-to-all-done.2
  93.3 0.2 convert.1
  93.5 0.2 convert_reduce_fusion
  93.7 3.1 %fusion.2 = bf16[64,8,8,128]{3,0,2,1:T(8,128)(2,1)S(1)} fusion(f32[64,8,8,128]{3,2,1,0:T(8,128)S(1)} %convert.1, f32[8,8,128]{2,1,0:T(8,128)S(1)} %broadcast_multiply_fusion, f32[8,64,64]{2,1,0:T(8,128)S(1)} %reshape.68), kind=kOutput, calls=%fused_computation.5 | convolution fusion | flops 403701760 | bytes 3309568 | tf_op jit(solution)/shard_map/mslc,smn->nslc/dot_general | solution.py:31
  96.8 0.7 copy.48
  97.5 40.6 %all_to_all.45 = bf16[64,8,8,128]{3,2,1,0:T(8,128)(2,1)S(1)} all-to-all(bf16[64,8,8,128]{3,2,1,0:T(8,128)(2,1)S(1)} %copy.48), channel_id=1, replica_groups=mesh['member'=64,'space'=8] {'member'}, dimensions={0} | all-to-all | bytes 2097152 | tf_op jit(solution)/shard_map/all_to_all | solution.py:94
  138.1 1.0 copy.70
  (8 shorter events, 0.1 us)
Async XLA Ops:
  0.0 16.5 %copy-start = (s32[512,8]{0,1:T(8,128)S(1)}, s32[512,8]{0,1:T(8,128)}, u32[]{:S(2)}) copy-start(s32[512,8]{0,1:T(8,128)} %param.15) | copy-start | bytes 49156
  0.0 29.3 %all-to-all-start = ((f32[1,512,128]{2,0,1:T(1,128)}), f32[1,512,128]{2,0,1:T(1,128)S(1)}, u32[]{:S(2)}, u32[]{:S(2)}) async-start(f32[1,512,128]{2,0,1:T(1,128)} %bitcast.29), calls=%async_computation | async-start | bytes 524288 | tf_op jit(solution)/shard_map/all_to_all | solution.py:52
  29.3 18.2 %all-to-all-start.1 = ((f32[1,512,128]{2,0,1:T(1,128)}), f32[1,512,128]{2,0,1:T(1,128)S(1)}, u32[]{:S(2)}, u32[]{:S(2)}) async-start(f32[1,512,128]{2,0,1:T(1,128)} %bitcast.3), calls=%async_computation.1 | async-start | bytes 524288 | tf_op jit(solution)/shard_map/all_to_all | solution.py:55
  47.5 37.7 %copy-start.1 = (s32[4096]{0:T(1024)S(1)}, s32[4096]{0:T(1024)}, u32[]{:S(2)}) copy-start(s32[4096]{0:T(1024)} %param.14) | copy-start | bytes 49156
  47.5 45.8 %all-to-all-start.2 = ((bf16[1,512,8,128]{3,2,0,1:T(8,128)(2,1)}), bf16[1,512,8,128]{3,2,0,1:T(8,128)(2,1)S(1)}, u32[]{:S(2)}, u32[]{:S(2)}) async-start(bf16[1,512,8,128]{3,2,0,1:T(8,128)(2,1)} %bitcast.7), calls=%async_computation.2 | async-start | bytes 2097152 | tf_op jit(solution)/shard_map/all_to_all | solution.py:93
  53.2 20.2 %collective-permute-start = (f32[1,1,8,4096]{3,2,1,0:T(8,128)S(1)}, f32[1,1,8,4096]{3,2,1,0:T(8,128)S(1)}, u32[]{:S(2)}, u32[]{:S(2)}) collective-permute-start(f32[1,1,8,4096]{3,2,1,0:T(8,128)S(1)} %reshape.66), channel_id=1, source_target_pairs={{0,8},{8,16},{16,24},{24,32},{32,40},{40,48},{48,56},{56,64},{64,7... | collective-permute-start | bytes 393224 | tf_op jit(solution)/shard_map/ppermute | solution.py:19
  56.2 21.3 %collective-permute-start.1 = (f32[1,1,8,4096]{3,2,1,0:T(8,128)S(1)}, f32[1,1,8,4096]{3,2,1,0:T(8,128)S(1)}, u32[]{:S(2)}, u32[]{:S(2)}) collective-permute-start(f32[1,1,8,4096]{3,2,1,0:T(8,128)S(1)} %reshape.66), channel_id=1, source_target_pairs={{8,0},{16,8},{24,16},{32,24},{40,32},{48,40},{56,48},{64,56},{72,6... | collective-permute-start | bytes 393224 | tf_op jit(solution)/shard_map/ppermute | solution.py:21
  77.6 10.4 %collective-permute-start.2 = (f32[3,1,8,4096]{3,2,1,0:T(8,128)S(1)}, f32[3,1,8,4096]{3,2,1,0:T(8,128)S(1)}, u32[]{:S(2)}, u32[]{:S(2)}) collective-permute-start(f32[3,1,8,4096]{3,2,1,0:T(8,128)S(1)} %constant_dynamic-update-slice_fusion), channel_id=1, source_target_pairs={{0,1},{1,2},{2,3},{3,4},{4,5},{5,6},{6,7},{8,9},{9,10},{10,11},{11... | collective-permute-start | bytes 1179656 | tf_op jit(solution)/shard_map/ppermute | solution.py:19
  83.3 9.1 %collective-permute-start.3 = (f32[3,1,8,4096]{3,2,1,0:T(8,128)S(1)}, f32[3,1,8,4096]{3,2,1,0:T(8,128)S(1)}, u32[]{:S(2)}, u32[]{:S(2)}) collective-permute-start(f32[3,1,8,4096]{3,2,1,0:T(8,128)S(1)} %constant_dynamic-update-slice_fusion), channel_id=1, source_target_pairs={{1,0},{2,1},{3,2},{4,3},{5,4},{6,5},{7,6},{9,8},{10,9},{11,10},{12... | collective-permute-start | bytes 1179656 | tf_op jit(solution)/shard_map/ppermute | solution.py:21
where the time goes:
time: 140 us; the launch traced here: 139 us
  waiting for transfers between devices  47.8 us (34%)
  blocking collectives  40.6 us (29%)
  starting transfers between devices  38.9 us (28%)
  matrix products  4.36 us (3%)
  local copies, waits for them, and re-layouts  3.74 us (3%)
  other arithmetic  3.47 us (2%)
    all_to_all x1, blocking collectives, local(): lax.all_to_all(increments(gathered_lines, mixing), 'member', split_axis=0...  40.6 us
    ppermute x2, waiting for transfers between devices, padded_2(): lax.ppermute(tail, axis, [(i, (i + 1) % count) for i in range(ends)])  17.6 us
    all_to_all x1, starting transfers between devices, local(): lax.all_to_all(replica_predicted_readings, 'member', split_axis=1, concat...  16.4 us
    all_to_all x1, waiting for transfers between devices, local(): lax.all_to_all(residual_mismatch, 'member', split_axis=1, concat_axis=0,...  11.7 us
    all_to_all x1, waiting for transfers between devices, local(): lax.all_to_all(replica_predicted_readings, 'member', split_axis=1, concat...  9.99 us
    ppermute x2, starting transfers between devices, padded_2(): lax.ppermute(tail, axis, [(i, (i + 1) % count) for i in range(ends)])  8.62 us
    ppermute x2, waiting for transfers between devices, padded_2(): lax.ppermute(head, axis, [((i + 1) % count, i) for i in range(ends)])  8.53 us
    all_to_all x1, starting transfers between devices, local(): lax.all_to_all(residual_mismatch, 'member', split_axis=1, concat_axis=0,...  5.67 us
  transfers between devices with their start and end apart: 7, of which 6 were waited for; matrix products, arithmetic and copies ran while one was open for 5% of the time, Pallas kernels for 0%

commit v1 on v0

v1 whole, which is shorter than its diff:
```python
import jax
import jax.numpy as jnp
from jax import lax
from jax.experimental import pallas as pl
from jax.experimental.pallas import tpu as pltpu
from jax.sharding import PartitionSpec as P

MESH = pl.DeviceIdType.MESH
SIDE = 8
MEMBERS = 64
STRIPS = 8
BLOCKS = 8
LEVELS = 8
CELLS = 128
CHUNK = 4
F32 = jnp.float32
BF16 = jnp.bfloat16


def far_first():
    def span(a):
        return min(a, SIDE - a)

    def rank(offset):
        a, b = span(offset[0]), span(offset[1])
        return (-(a + b), -max(a, b), min(offset))

    offsets = [(a, b) for a in range(SIDE) for b in range(SIDE) if (a, b) != (0, 0)]
    return sorted(offsets, key=rank)


OFFSETS = far_first()


def kernel(
    prior,
    model,
    noise,
    sensor,
    power,
    tally,
    select,
    out,
    got_model,
    got_noise,
    got_prior,
    mine_sensor,
    mine_power,
    products,
    partial,
    got_partial,
    mixing,
    wide_in,
    wide_out,
    increment,
    send_sems,
    recv_sems,
    local_sems,
    strip_sems,
    line_sems,
):
    me = lax.axis_index("member")
    strip = lax.axis_index("space")
    row, column = me // SIDE, lax.rem(me, SIDE)

    def member(offset):
        return lax.rem(row + offset[0], SIDE) * SIDE + lax.rem(column + offset[1], SIDE)

    peers = [member(offset) for offset in OFFSETS]
    east, west = lax.rem(strip + 1, STRIPS), lax.rem(strip + STRIPS - 1, STRIPS)
    north, south = lax.rem(me + 1, MEMBERS), lax.rem(me + MEMBERS - 1, MEMBERS)

    own = [
        pltpu.make_async_copy(
            sensor.at[pl.ds(me * BLOCKS, BLOCKS)], mine_sensor, local_sems.at[0]
        ),
        pltpu.make_async_copy(
            power.at[pl.ds(me * BLOCKS, BLOCKS)], mine_power, local_sems.at[1]
        ),
        pltpu.make_async_copy(
            model.at[0, pl.ds(me * BLOCKS, BLOCKS)], got_model.at[me], local_sems.at[2]
        ),
        pltpu.make_async_copy(
            noise.at[0, pl.ds(me * BLOCKS, BLOCKS)], got_noise.at[me], local_sems.at[3]
        ),
        pltpu.make_async_copy(
            prior.at[0, pl.ds(me * BLOCKS, BLOCKS)], got_prior.at[me], local_sems.at[4]
        ),
    ]
    for copy in own:
        copy.start()

    barrier = pltpu.get_barrier_semaphore()
    for peer in peers:
        pl.semaphore_signal(barrier, inc=1, device_id=(peer, strip), device_id_type=MESH)
    for beside in (east, west):
        pl.semaphore_signal(barrier, inc=1, device_id=(me, beside), device_id_type=MESH)
    pl.semaphore_wait(barrier, len(peers) + 2)

    def push(src, dst, sem, peer, beside):
        pltpu.make_async_remote_copy(
            src_ref=src,
            dst_ref=dst,
            send_sem=send_sems.at[sem],
            recv_sem=recv_sems.at[sem],
            device_id=(peer, beside),
            device_id_type=MESH,
        ).start()

    for peer in peers:
        push(model.at[0, pl.ds(peer * BLOCKS, BLOCKS)], got_model.at[me], 0, peer, strip)
        push(noise.at[0, pl.ds(peer * BLOCKS, BLOCKS)], got_noise.at[me], 1, peer, strip)

    def push_prior(chunk):
        for peer in peers:
            push(
                prior.at[0, pl.ds(peer * BLOCKS + chunk * CHUNK, CHUNK)],
                got_prior.at[me, pl.ds(chunk * CHUNK, CHUNK)],
                2 + chunk,
                peer,
                strip,
            )

    push_prior(0)

    def wait_all(sems, sem, ref):
        pltpu.make_async_copy(ref, ref, sems.at[sem]).wait()

    for copy in own:
        copy.wait()
    others = pl.ds(0, MEMBERS - 1)
    wait_all(recv_sems, 0, got_model.at[others])
    wait_all(recv_sems, 1, got_noise.at[others])

    slots = lax.broadcasted_iota(jnp.int32, (1, CELLS), 1)
    for block in range(BLOCKS):
        forecast = got_model[:, block, :]
        drawn = got_noise[:, block, :]
        mismatch = mine_sensor[block : block + 1, :] + drawn - forecast
        anomaly = forecast - jnp.sum(forecast, axis=0, keepdims=True) / MEMBERS
        spread = jnp.sum(anomaly * anomaly, axis=0, keepdims=True) / (MEMBERS - 1)
        active = (slots < tally[me * BLOCKS + block]).astype(F32)
        weights = mismatch * (active / (spread + mine_power[block : block + 1, :]))
        product = lax.dot_general(
            weights,
            anomaly,
            (((1,), (1,)), ((), ())),
            precision=lax.Precision.HIGHEST,
            preferred_element_type=F32,
        )
        half = (block % 2) * MEMBERS
        products[1, block // 2, :, half : half + MEMBERS] = product

    def beside_copy(slot, beside):
        return pltpu.make_async_remote_copy(
            src_ref=products.at[1],
            dst_ref=products.at[slot],
            send_sem=strip_sems.at[0, slot // 2],
            recv_sem=strip_sems.at[1, slot // 2],
            device_id=(me, beside),
            device_id_type=MESH,
        )

    copies = [beside_copy(0, east), beside_copy(2, west)]
    for copy in copies:
        copy.start()
    for copy in copies:
        copy.wait()

    low = lax.broadcasted_iota(jnp.int32, (MEMBERS, CELLS), 1) < MEMBERS

    def part_of(tile, pair):
        folded = []
        for item in range(2):
            first = ((tile * BLOCKS) + pair * 2 + item) * 3 * BLOCKS
            total = jnp.zeros((MEMBERS, CELLS), F32)
            for beside in range(3):
                for both in range(BLOCKS // 2):
                    at = first + beside * BLOCKS + both * 2
                    total = total + products[beside, both] * jnp.where(low, select[at], select[at + 1])
            folded.append(total + pltpu.roll(total, MEMBERS, 1))
        return jnp.where(low, folded[0], folded[1])

    def fill(tile):
        def body(pair, carry):
            partial[tile, pair] = part_of(tile, pair)
            return carry

        lax.fori_loop(0, BLOCKS // 2, body, 0)

    def line_copy(tile, slot, peer):
        return pltpu.make_async_remote_copy(
            src_ref=partial.at[tile],
            dst_ref=got_partial.at[slot],
            send_sem=line_sems.at[0, slot],
            recv_sem=line_sems.at[1, slot],
            device_id=(peer, strip),
            device_id_type=MESH,
        )

    fill(0)
    down = line_copy(0, 0, south)
    down.start()
    fill(2)
    up = line_copy(2, 1, north)
    up.start()
    push_prior(1)
    fill(1)
    down.wait()
    up.wait()

    for pair in range(BLOCKS // 2):
        both = partial[1, pair] + got_partial[0, pair] + got_partial[1, pair]
        for item in range(2):
            one = both if item == 0 else pltpu.roll(both, MEMBERS, 1)
            one = one[:, 0:MEMBERS]
            one = one - jnp.sum(one, axis=1, keepdims=True) / MEMBERS
            high = one.astype(BF16)
            rest = one - high.astype(F32)
            middle = rest.astype(BF16)
            rest = rest - middle.astype(F32)
            mixing[pair * 2 + item, 0] = high
            mixing[pair * 2 + item, 1] = middle
            mixing[pair * 2 + item, 2] = rest.astype(BF16)

    for chunk in range(BLOCKS // CHUNK):
        wait_all(recv_sems, 2 + chunk, got_prior.at[others, pl.ds(0, CHUNK)])

        def body(step, carry):
            block = chunk * CHUNK + step
            wide_in[...] = got_prior[:, block].astype(F32).reshape(MEMBERS * LEVELS, CELLS)
            state = jnp.concatenate(
                [
                    wide_in[pl.ds(level, MEMBERS, stride=LEVELS), :].astype(BF16)
                    for level in range(LEVELS)
                ],
                axis=1,
            )
            total = jnp.zeros((MEMBERS, LEVELS * CELLS), F32)
            for term in (2, 1, 0):
                total = total + jnp.dot(mixing[block, term], state, preferred_element_type=F32)
            for level in range(LEVELS):
                wide_out[pl.ds(level, MEMBERS, stride=LEVELS), :] = total[
                    :, level * CELLS : (level + 1) * CELLS
                ]
            increment[:, block] = wide_out[...].reshape(MEMBERS, LEVELS, CELLS).astype(BF16)
            return carry

        lax.fori_loop(0, CHUNK, body, 0)
        part = pl.ds(chunk * CHUNK, CHUNK)
        landing = pl.ds(me * BLOCKS + chunk * CHUNK, CHUNK)
        for peer in peers:
            push(increment.at[peer, part], out.at[0, landing], 4 + chunk, peer, strip)
        pltpu.make_async_copy(
            increment.at[me, part], out.at[0, landing], local_sems.at[5 + chunk]
        ).start()

    for chunk in range(BLOCKS // CHUNK):
        part = pl.ds(chunk * CHUNK, CHUNK)
        landing = pl.ds(me * BLOCKS + chunk * CHUNK, CHUNK)
        pltpu.make_async_copy(
            increment.at[me, part], out.at[0, landing], local_sems.at[5 + chunk]
        ).wait()
    wait_all(send_sems, 0, got_model.at[others])
    wait_all(send_sems, 1, got_noise.at[others])
    for chunk in range(BLOCKS // CHUNK):
        for sem, sems in ((2 + chunk, (send_sems,)), (4 + chunk, (send_sems, recv_sems))):
            for each in sems:
                wait_all(each, sem, increment.at[others, pl.ds(0, CHUNK)])


def selection(neighbour_listing, sensor_patch_start):
    me = lax.axis_index("member")
    strip = lax.axis_index("space")
    around = jnp.arange(-1, 2, dtype=jnp.int32)
    tiles = neighbour_listing.reshape(MEMBERS, BLOCKS * BLOCKS)
    listed = jnp.concatenate(
        [
            lax.dynamic_slice_in_dim(tiles, lax.rem(me + shift + MEMBERS, MEMBERS), 1, 0)
            for shift in (-1, 0, 1)
        ]
    ).reshape(3, BLOCKS, 1, 1, BLOCKS)
    starts = lax.dynamic_slice_in_dim(
        sensor_patch_start.reshape(STRIPS, MEMBERS, BLOCKS), me, 1, 1
    )[:, 0]
    starts = jnp.concatenate(
        [
            lax.dynamic_slice_in_dim(starts, lax.rem(strip + shift + STRIPS, STRIPS), 1, 0)
            for shift in (-1, 0, 1)
        ]
    )[None, None]
    inner = jnp.arange(BLOCKS, dtype=jnp.int32)
    names = ((strip + around)[:, None] * MEMBERS + me) * BLOCKS + inner[None]
    hits = jnp.sum((listed == names[None, None, :, :, None]).astype(F32), axis=-1)
    delta_x = (strip * BLOCKS + inner)[None, :, None, None] - starts
    delta_x = delta_x.astype(F32)
    delta_y = around[:, None, None, None].astype(F32)
    distance = delta_x * delta_x + delta_y * delta_y
    taper = 1.0 / (1.0 + distance / float(BLOCKS * BLOCKS))
    return (taper * hits / (MEMBERS - 1)).reshape(-1)


def local(prior, model, noise, sensor, power, tally, start, listing):
    vmem, smem, anywhere = pltpu.VMEM, pltpu.SMEM, pl.ANY
    tile = (MEMBERS, BLOCKS, CELLS)
    state = (MEMBERS, BLOCKS, LEVELS, CELLS)
    packed = (BLOCKS // 2, MEMBERS, CELLS)
    dma = pltpu.SemaphoreType.DMA
    return pl.pallas_call(
        kernel,
        name="analysis",
        out_shape=jax.ShapeDtypeStruct(prior.shape, BF16),
        in_specs=[pl.BlockSpec(memory_space=anywhere)] * 5 + [pl.BlockSpec(memory_space=smem)] * 2,
        out_specs=pl.BlockSpec(memory_space=vmem),
        scratch_shapes=[
            vmem(tile, F32),
            vmem(tile, F32),
            vmem(state, BF16),
            vmem((BLOCKS, CELLS), F32),
            vmem((BLOCKS, CELLS), F32),
            vmem((3, *packed), F32),
            vmem((3, *packed), F32),
            vmem((2, *packed), F32),
            vmem((BLOCKS, 3, MEMBERS, MEMBERS), BF16),
            vmem((MEMBERS * LEVELS, CELLS), F32),
            vmem((MEMBERS * LEVELS, CELLS), F32),
            vmem(state, BF16),
            dma((6,)),
            dma((6,)),
            dma((7,)),
            dma((2, 2)),
            dma((2, 2)),
        ],
        compiler_params=pltpu.CompilerParams(collective_id=0, has_side_effects=True),
    )(prior, model, noise, sensor, power, tally, selection(listing, start))


def solution(mesh):
    placed = (
        P("member", "space", None, None),
        P("member", "space", None),
        P("member", "space", None),
        P("space", None),
        P("space", None),
        P("space"),
        P(),
        P("space", None),
    )
    return jax.shard_map(
        local,
        mesh=mesh,
        in_specs=placed,
        out_specs=P("member", "space", None, None),
        check_vma=False,
    )
```

time: 140 us -> 88.2 us (0.63)
  the two profiles are of different devices: /device:TPU:3 before, /device:TPU:1 now
where the time goes in v1:
time: 88.2 us; the launch traced here: 87.4 us
  Pallas kernels  82.1 us (93%)
  local copies, waits for them, and re-layouts  4.67 us (5%)
    pallas_call x1, Pallas kernels, local(): pl.pallas_call(kernel, name='analysis', out_shape=jax.ShapeDtypeStruct(pr...  82.1 us
    unnamed x6, local copies, waits for them, and re-layouts  3.59 us

profile of v1, /device:TPU:1, one launch (start us, length us, event | category | flops | bytes accessed | tf_op | source)
XLA Modules:
  0.0 87.4 jit_solution(8267653334037121718)
XLA Ops:
  0.0 0.0 copy-start
  0.0 0.1 iota_add_fusion
  0.1 0.6 copy-done
  0.7 0.2 reshape.78
  0.9 0.0 copy-start.1
  0.9 0.1 convert_multiply_fusion
  1.0 0.6 copy-done.1
  1.6 0.1 copy.10
  1.7 0.1 reshape.79
  1.9 0.1 eq.15
  2.0 0.2 convert_reduce_fusion
  2.2 0.1 fusion
  2.3 0.7 reshape.82.select
  3.0 82.1 %analysis.1 = bf16[1,512,8,128]{3,2,1,0:T(8,128)(2,1)} custom-call(bf16[1,512,8,128]{3,2,1,0:T(8,128)(2,1)} %prior.1, f32[1,512,128]{2,1,0:T(8,128)} %model.1, f32[1,512,128]{2,1,0:T(8,128)} %noise.1, f32[512,128]{1,0:T(8,128)} %sensor.1, f32[512,128]{1,0:T(8,128)} %power.1, s32[512]{0:T(512)} %tally.1, f32[576]{0:T(1024)} %reshape.82.select), custom_call_target="tpu_custom_call" | custom-call | tf_op jit(solution)/shard_map/analysis/pallas_call | solution.py:309
  85.2 2.3 %copy.12 = bf16[1,512,8,128]{3,2,1,0:T(8,128)(2,1)} copy(bf16[1,512,8,128]{3,2,1,0:T(8,128)(2,1)} %analysis.1) | data formatting | bytes 2097152
  (7 shorter events, 0.1 us)
Async XLA Ops:
  0.0 0.7 copy-start
  0.9 0.7 copy-start.1

commit v2 on v1

--- a/solution.py
+++ b/solution.py
@@ -12,7 +12,11 @@
 BLOCKS = 8
 LEVELS = 8
 CELLS = 128
-CHUNK = 4
+CHUNK = 2
+CHUNKS = BLOCKS // CHUNK
+EARLY = 2
+BEFORE = 3
+ACROSS = (4, 3, 5, 2, 6, 1, 7, 0)
 F32 = jnp.float32
 BF16 = jnp.bfloat16
 
@@ -38,14 +42,19 @@
     noise,
     sensor,
     power,
-    tally,
-    select,
+    tally_hbm,
+    start_hbm,
+    listing_hbm,
     out,
     got_model,
     got_noise,
     got_prior,
     mine_sensor,
     mine_power,
+    listing,
+    tally,
+    start,
+    pattern,
     products,
     partial,
     got_partial,
@@ -58,6 +67,7 @@
     local_sems,
     strip_sems,
     line_sems,
+    row_sems,
 ):
     me = lax.axis_index("member")
     strip = lax.axis_index("space")
@@ -69,33 +79,31 @@
     peers = [member(offset) for offset in OFFSETS]
     east, west = lax.rem(strip + 1, STRIPS), lax.rem(strip + STRIPS - 1, STRIPS)
     north, south = lax.rem(me + 1, MEMBERS), lax.rem(me + MEMBERS - 1, MEMBERS)
-
-    own = [
-        pltpu.make_async_copy(
-            sensor.at[pl.ds(me * BLOCKS, BLOCKS)], mine_sensor, local_sems.at[0]
-        ),
-        pltpu.make_async_copy(
-            power.at[pl.ds(me * BLOCKS, BLOCKS)], mine_power, local_sems.at[1]
-        ),
-        pltpu.make_async_copy(
-            model.at[0, pl.ds(me * BLOCKS, BLOCKS)], got_model.at[me], local_sems.at[2]
-        ),
-        pltpu.make_async_copy(
-            noise.at[0, pl.ds(me * BLOCKS, BLOCKS)], got_noise.at[me], local_sems.at[3]
-        ),
-        pltpu.make_async_copy(
-            prior.at[0, pl.ds(me * BLOCKS, BLOCKS)], got_prior.at[me], local_sems.at[4]
-        ),
-    ]
-    for copy in own:
-        copy.start()
 
     barrier = pltpu.get_barrier_semaphore()
     for peer in peers:
         pl.semaphore_signal(barrier, inc=1, device_id=(peer, strip), device_id_type=MESH)
     for beside in (east, west):
         pl.semaphore_signal(barrier, inc=1, device_id=(me, beside), device_id_type=MESH)
-    pl.semaphore_wait(barrier, len(peers) + 2)
+
+    mine = pl.ds(me * BLOCKS, BLOCKS)
+    own = [
+        pltpu.make_async_copy(src, dst, local_sems.at[at])
+        for at, (src, dst) in enumerate(
+            (
+                (start_hbm, start),
+                (tally_hbm, tally),
+                (listing_hbm, listing),
+                (sensor.at[mine], mine_sensor),
+                (power.at[mine], mine_power),
+                (model.at[0, mine], got_model.at[me]),
+                (noise.at[0, mine], got_noise.at[me]),
+                (prior.at[0, mine], got_prior.at[me]),
+            )
+        )
+    ]
+    for copy in own:
+        copy.start()
 
     def push(src, dst, sem, peer, beside):
         pltpu.make_async_remote_copy(
@@ -107,30 +115,101 @@
             device_id_type=MESH,
         ).start()
 
+    def push_readings(peer):
+        theirs = pl.ds(peer * BLOCKS, BLOCKS)
+        push(model.at[0, theirs], got_model.at[me], 0, peer, strip)
+        push(noise.at[0, theirs], got_noise.at[me], 1, peer, strip)
+
+    def push_prior(chunk, peer):
+        push(
+            prior.at[0, pl.ds(peer * BLOCKS + chunk * CHUNK, CHUNK)],
+            got_prior.at[me, pl.ds(chunk * CHUNK, CHUNK)],
+            2 + chunk,
+            peer,
+            strip,
+        )
+
+    def early(peer):
+        for chunk in range(EARLY):
+            push_prior(chunk, peer)
+
+    def to_row(target, *actions):
+        for shift in ACROSS:
+            peer = target * SIDE + lax.rem(column + shift, SIDE)
+
+            def act(peer=peer):
+                for action in actions:
+                    action(peer)
+
+            if shift == 0:
+                pl.when(target != row)(act)
+            else:
+                act()
+
+    pl.semaphore_wait(barrier, len(peers) + 2)
+
+    def there(action):
+        def body(at, carry):
+            to_row(row - at, action)
+            return carry
+
+        lax.fori_loop(0, row + 1, body, 0)
+
     for peer in peers:
-        push(model.at[0, pl.ds(peer * BLOCKS, BLOCKS)], got_model.at[me], 0, peer, strip)
-        push(noise.at[0, pl.ds(peer * BLOCKS, BLOCKS)], got_noise.at[me], 1, peer, strip)
-
-    def push_prior(chunk):
+        push_readings(peer)
+    for chunk in range(EARLY):
         for peer in peers:
-            push(
-                prior.at[0, pl.ds(peer * BLOCKS + chunk * CHUNK, CHUNK)],
-                got_prior.at[me, pl.ds(chunk * CHUNK, CHUNK)],
-                2 + chunk,
-                peer,
-                strip,
-            )
-
-    push_prior(0)
+            push_prior(chunk, peer)
 
     def wait_all(sems, sem, ref):
         pltpu.make_async_copy(ref, ref, sems.at[sem]).wait()
 
     for copy in own:
         copy.wait()
+
+    around = 3 * BLOCKS
+    tall, long = (around, CELLS), (around, MEMBERS * BLOCKS)
+    which = lax.broadcasted_iota(jnp.int32, tall, 0)
+    begins = jnp.zeros(tall, jnp.int32)
+    for at in range(around):
+        tile = lax.rem(strip + at // BLOCKS + STRIPS - 1, STRIPS) * MEMBERS + me
+        begins = jnp.where(which == at, start[tile * BLOCKS + at % BLOCKS], begins)
+    begins = jnp.concatenate([begins] * (MEMBERS * BLOCKS // CELLS), axis=1)
+    which = lax.broadcasted_iota(jnp.int32, long, 0)
+    state = lax.broadcasted_iota(jnp.int32, long, 1)
+    names = ((strip + (which >> 3) - 1) * MEMBERS + me) * BLOCKS + (which & 7)
+    hits = jnp.zeros(long, F32)
+    for at in range(BLOCKS):
+        hits = hits + jnp.where(listing[at : at + 1, :] == names, 1.0, 0.0)
+    delta_x = (strip * BLOCKS + (state & 7) - begins).astype(F32)
+    delta_y = ((state >> 3) - me).astype(F32)
+    distance = delta_x * delta_x + delta_y * delta_y
+    taper = hits * (1.0 / (1.0 + distance * (1.0 / (BLOCKS * BLOCKS)))) * (1.0 / (MEMBERS - 1))
+    tile = me + (which >> 3) - 1
+    tile = jnp.where(tile < 0, tile + MEMBERS, jnp.where(tile >= MEMBERS, tile - MEMBERS, tile))
+    chosen = (state == tile * BLOCKS + (which & 7)).astype(F32)
+    factors = lax.dot_general(
+        chosen,
+        taper,
+        (((1,), (1,)), ((), ())),
+        precision=lax.Precision.HIGHEST,
+        preferred_element_type=F32,
+    )
+    spread_to = (around, around * MEMBERS)
+    lanes = lax.broadcasted_iota(jnp.int32, spread_to, 1) >> 6
+    place = (lax.broadcasted_iota(jnp.int32, spread_to, 0) == lanes).astype(F32)
+    spread_out = jnp.dot(
+        factors, place, precision=lax.Precision.HIGHEST, preferred_element_type=F32
+    )
+    for both in range(around // 2):
+        pattern[:, both, :] = spread_out[:, both * CELLS : (both + 1) * CELLS]
+
     others = pl.ds(0, MEMBERS - 1)
     wait_all(recv_sems, 0, got_model.at[others])
     wait_all(recv_sems, 1, got_noise.at[others])
+    for peer in peers:
+        for chunk in range(EARLY, BEFORE):
+            push_prior(chunk, peer)
 
     slots = lax.broadcasted_iota(jnp.int32, (1, CELLS), 1)
     for block in range(BLOCKS):
@@ -172,12 +251,11 @@
     def part_of(tile, pair):
         folded = []
         for item in range(2):
-            first = ((tile * BLOCKS) + pair * 2 + item) * 3 * BLOCKS
+            at = tile * BLOCKS + pair * 2 + item
             total = jnp.zeros((MEMBERS, CELLS), F32)
-            for beside in range(3):
-                for both in range(BLOCKS // 2):
-                    at = first + beside * BLOCKS + both * 2
-                    total = total + products[beside, both] * jnp.where(low, select[at], select[at + 1])
+            for both in range(around // 2):
+                factor = pattern[at, both : both + 1, :]
+                total = total + products[both // (BLOCKS // 2), both % (BLOCKS // 2)] * factor
             folded.append(total + pltpu.roll(total, MEMBERS, 1))
         return jnp.where(low, folded[0], folded[1])
 
@@ -204,7 +282,9 @@
     fill(2)
     up = line_copy(2, 1, north)
     up.start()
-    push_prior(1)
+    for peer in peers:
+        for chunk in range(BEFORE, CHUNKS):
+            push_prior(chunk, peer)
     fill(1)
     down.wait()
     up.wait()
@@ -223,7 +303,14 @@
             mixing[pair * 2 + item, 1] = middle
             mixing[pair * 2 + item, 2] = rest.astype(BF16)
 
-    for chunk in range(BLOCKS // CHUNK):
+    def landed(chunk):
+        return pltpu.make_async_copy(
+            increment.at[me, pl.ds(chunk * CHUNK, CHUNK)],
+            out.at[0, pl.ds(me * BLOCKS + chunk * CHUNK, CHUNK)],
+            local_sems.at[8 + chunk],
+        )
+
+    for chunk in range(CHUNKS):
         wait_all(recv_sems, 2 + chunk, got_prior.at[others, pl.ds(0, CHUNK)])
 
         def body(step, carry):
@@ -250,54 +337,18 @@
         part = pl.ds(chunk * CHUNK, CHUNK)
         landing = pl.ds(me * BLOCKS + chunk * CHUNK, CHUNK)
         for peer in peers:
-            push(increment.at[peer, part], out.at[0, landing], 4 + chunk, peer, strip)
-        pltpu.make_async_copy(
-            increment.at[me, part], out.at[0, landing], local_sems.at[5 + chunk]
-        ).start()
-
-    for chunk in range(BLOCKS // CHUNK):
-        part = pl.ds(chunk * CHUNK, CHUNK)
-        landing = pl.ds(me * BLOCKS + chunk * CHUNK, CHUNK)
-        pltpu.make_async_copy(
-            increment.at[me, part], out.at[0, landing], local_sems.at[5 + chunk]
-        ).wait()
+            push(increment.at[peer, part], out.at[0, landing], 2 + CHUNKS + chunk, peer, strip)
+        landed(chunk).start()
+
+    for chunk in range(CHUNKS):
+        landed(chunk).wait()
     wait_all(send_sems, 0, got_model.at[others])
     wait_all(send_sems, 1, got_noise.at[others])
-    for chunk in range(BLOCKS // CHUNK):
-        for sem, sems in ((2 + chunk, (send_sems,)), (4 + chunk, (send_sems, recv_sems))):
-            for each in sems:
-                wait_all(each, sem, increment.at[others, pl.ds(0, CHUNK)])
-
-
-def selection(neighbour_listing, sensor_patch_start):
-    me = lax.axis_index("member")
-    strip = lax.axis_index("space")
-    around = jnp.arange(-1, 2, dtype=jnp.int32)
-    tiles = neighbour_listing.reshape(MEMBERS, BLOCKS * BLOCKS)
-    listed = jnp.concatenate(
-        [
-            lax.dynamic_slice_in_dim(tiles, lax.rem(me + shift + MEMBERS, MEMBERS), 1, 0)
-            for shift in (-1, 0, 1)
-        ]
-    ).reshape(3, BLOCKS, 1, 1, BLOCKS)
-    starts = lax.dynamic_slice_in_dim(
-        sensor_patch_start.reshape(STRIPS, MEMBERS, BLOCKS), me, 1, 1
-    )[:, 0]
-    starts = jnp.concatenate(
-        [
-            lax.dynamic_slice_in_dim(starts, lax.rem(strip + shift + STRIPS, STRIPS), 1, 0)
-            for shift in (-1, 0, 1)
-        ]
-    )[None, None]
-    inner = jnp.arange(BLOCKS, dtype=jnp.int32)
-    names = ((strip + around)[:, None] * MEMBERS + me) * BLOCKS + inner[None]
-    hits = jnp.sum((listed == names[None, None, :, :, None]).astype(F32), axis=-1)
-    delta_x = (strip * BLOCKS + inner)[None, :, None, None] - starts
-    delta_x = delta_x.astype(F32)
-    delta_y = around[:, None, None, None].astype(F32)
-    distance = delta_x * delta_x + delta_y * delta_y
-    taper = 1.0 / (1.0 + distance / float(BLOCKS * BLOCKS))
-    return (taper * hits / (MEMBERS - 1)).reshape(-1)
+    one = increment.at[others, pl.ds(0, CHUNK)]
+    for chunk in range(CHUNKS):
+        wait_all(send_sems, 2 + chunk, one)
+        wait_all(send_sems, 2 + CHUNKS + chunk, one)
+        wait_all(recv_sems, 2 + CHUNKS + chunk, one)
 
 
 def local(prior, model, noise, sensor, power, tally, start, listing):
@@ -309,8 +360,8 @@
     return pl.pallas_call(
         kernel,
         name="analysis",
-        out_shape=jax.ShapeDtypeStruct(prior.shape, BF16),
-        in_specs=[pl.BlockSpec(memory_space=anywhere)] * 5 + [pl.BlockSpec(memory_space=smem)] * 2,
+        out_shape=vmem(prior.shape, BF16),
+        in_specs=[pl.BlockSpec(memory_space=anywhere)] * 8,
         out_specs=pl.BlockSpec(memory_space=vmem),
         scratch_shapes=[
             vmem(tile, F32),
@@ -318,6 +369,10 @@
             vmem(state, BF16),
             vmem((BLOCKS, CELLS), F32),
             vmem((BLOCKS, CELLS), F32),
+            vmem((BLOCKS, MEMBERS * BLOCKS), jnp.int32),
+            smem((MEMBERS * BLOCKS,), jnp.int32),
+            smem((STRIPS * MEMBERS * BLOCKS,), jnp.int32),
+            vmem((3 * BLOCKS, 3 * BLOCKS // 2, CELLS), F32),
             vmem((3, *packed), F32),
             vmem((3, *packed), F32),
             vmem((2, *packed), F32),
@@ -325,14 +380,15 @@
             vmem((MEMBERS * LEVELS, CELLS), F32),
             vmem((MEMBERS * LEVELS, CELLS), F32),
             vmem(state, BF16),
-            dma((6,)),
-            dma((6,)),
-            dma((7,)),
+            dma((2 + 2 * CHUNKS,)),
+            dma((2 + 2 * CHUNKS,)),
+            dma((8 + CHUNKS,)),
             dma((2, 2)),
             dma((2, 2)),
+            pltpu.SemaphoreType.REGULAR((SIDE,)),
         ],
         compiler_params=pltpu.CompilerParams(collective_id=0, has_side_effects=True),
-    )(prior, model, noise, sensor, power, tally, selection(listing, start))
+    )(prior, model, noise, sensor, power, tally, start, listing.T)
 
 
 def solution(mesh):

time: 88.2 us -> 79 us (0.90)
  Pallas kernels: 82.1 us -> 77.9 us
  local copies, waits for them, and re-layouts: 4.67 us -> 0.97 us
    pallas_call x1, Pallas kernels: 82.1 us -> 77.9 us  [local(): pl.pallas_call(kernel, name='analysis', out_shape=vmem(prior.shape, BF16)...]
    unnamed x6 -> x1, local copies, waits for them, and re-layouts: 3.59 us -> 0.97 us
where the time goes in v2:
time: 79 us; the launch traced here: 78.9 us
  Pallas kernels  77.9 us (99%)
  local copies, waits for them, and re-layouts  0.97 us (1%)
    pallas_call x1, Pallas kernels, local(): pl.pallas_call(kernel, name='analysis', out_shape=vmem(prior.shape, BF16)...  77.9 us

profile of v2, /device:TPU:1, one launch (start us, length us, event | category | flops | bytes accessed | tf_op | source)
XLA Modules:
  0.0 78.9 jit_solution(11260196015296747902)
XLA Ops:
  0.0 77.9 %analysis.1 = bf16[1,512,8,128]{3,2,1,0:T(8,128)(2,1)S(1)} custom-call(bf16[1,512,8,128]{3,2,1,0:T(8,128)(2,1)} %prior.1, f32[1,512,128]{2,1,0:T(8,128)} %model.1, f32[1,512,128]{2,1,0:T(8,128)} %noise.1, f32[512,128]{1,0:T(8,128)} %sensor.1, f32[512,128]{1,0:T(8,128)} %power.1, s32[512]{0:T(512)} %tally_hbm.1, s32[4096]{0:T(1024)} %start_hbm.1, ...), custom_call_target="tpu_custom_call" | custom-call | tf_op jit(solution)/shard_map/analysis/pallas_call | solution.py:360
  77.9 1.0 %copy.10 = bf16[1,512,8,128]{3,2,1,0:T(8,128)(2,1)} copy(bf16[1,512,8,128]{3,2,1,0:T(8,128)(2,1)S(1)} %analysis.1) | data formatting | bytes 2097152

commit v3 on v2

--- a/solution.py
+++ b/solution.py
@@ -14,9 +14,10 @@
 CELLS = 128
 CHUNK = 2
 CHUNKS = BLOCKS // CHUNK
-EARLY = 2
+EARLY = 3
 BEFORE = 3
-ACROSS = (4, 3, 5, 2, 6, 1, 7, 0)
+MODEL_STEPS = float(1 << 20)
+NOISE_STEPS = float(1 << 19)
 F32 = jnp.float32
 BF16 = jnp.bfloat16
 
@@ -46,6 +47,10 @@
     start_hbm,
     listing_hbm,
     out,
+    raw_model,
+    raw_noise,
+    coded,
+    got_coded,
     got_model,
     got_noise,
     got_prior,
@@ -67,7 +72,6 @@
     local_sems,
     strip_sems,
     line_sems,
-    row_sems,
 ):
     me = lax.axis_index("member")
     strip = lax.axis_index("space")
@@ -96,9 +100,9 @@
                 (listing_hbm, listing),
                 (sensor.at[mine], mine_sensor),
                 (power.at[mine], mine_power),
-                (model.at[0, mine], got_model.at[me]),
-                (noise.at[0, mine], got_noise.at[me]),
                 (prior.at[0, mine], got_prior.at[me]),
+                (model.at[0], raw_model),
+                (noise.at[0], raw_noise),
             )
         )
     ]
@@ -116,9 +120,7 @@
         ).start()
 
     def push_readings(peer):
-        theirs = pl.ds(peer * BLOCKS, BLOCKS)
-        push(model.at[0, theirs], got_model.at[me], 0, peer, strip)
-        push(noise.at[0, theirs], got_noise.at[me], 1, peer, strip)
+        push(coded.at[peer], got_coded.at[me], 0, peer, strip)
 
     def push_prior(chunk, peer):
         push(
@@ -129,32 +131,25 @@
             strip,
         )
 
-    def early(peer):
-        for chunk in range(EARLY):
-            push_prior(chunk, peer)
-
-    def to_row(target, *actions):
-        for shift in ACROSS:
-            peer = target * SIDE + lax.rem(column + shift, SIDE)
-
-            def act(peer=peer):
-                for action in actions:
-                    action(peer)
-
-            if shift == 0:
-                pl.when(target != row)(act)
-            else:
-                act()
+    for copy in own[-2:]:
+        copy.wait()
+
+    def encode(at, carry):
+        rows = pl.ds(at * CELLS, CELLS)
+        tiles = pl.ds(at * (CELLS // BLOCKS), CELLS // BLOCKS)
+        shape = (CELLS // BLOCKS, BLOCKS, CELLS)
+        first = jnp.floor(raw_model[rows, :] * MODEL_STEPS + 0.5).astype(jnp.int32)
+        second = jnp.floor(raw_noise[rows, :] * NOISE_STEPS + 0.5).astype(jnp.int32)
+        low = ((first & 255) << 8) + (second & 255) - 32768
+        for word, value in enumerate((first >> 8, second >> 8, low)):
+            coded[tiles, word] = value.reshape(shape).astype(jnp.int16)
+        return carry
+
+    lax.fori_loop(0, MEMBERS * BLOCKS // CELLS, encode, 0)
+    kept = pltpu.make_async_copy(coded.at[me], got_coded.at[me], local_sems.at[8 + CHUNKS])
+    kept.start()
 
     pl.semaphore_wait(barrier, len(peers) + 2)
-
-    def there(action):
-        def body(at, carry):
-            to_row(row - at, action)
-            return carry
-
-        lax.fori_loop(0, row + 1, body, 0)
-
     for peer in peers:
         push_readings(peer)
     for chunk in range(EARLY):
@@ -164,8 +159,9 @@
     def wait_all(sems, sem, ref):
         pltpu.make_async_copy(ref, ref, sems.at[sem]).wait()
 
-    for copy in own:
+    for copy in own[:-2]:
         copy.wait()
+    kept.wait()
 
     around = 3 * BLOCKS
     tall, long = (around, CELLS), (around, MEMBERS * BLOCKS)
@@ -205,11 +201,20 @@
         pattern[:, both, :] = spread_out[:, both * CELLS : (both + 1) * CELLS]
 
     others = pl.ds(0, MEMBERS - 1)
-    wait_all(recv_sems, 0, got_model.at[others])
-    wait_all(recv_sems, 1, got_noise.at[others])
+    wait_all(recv_sems, 0, got_coded.at[others])
     for peer in peers:
         for chunk in range(EARLY, BEFORE):
             push_prior(chunk, peer)
+
+    def decode(at, carry):
+        group = pl.ds(at * BLOCKS, BLOCKS)
+        first, second, low = (got_coded[group, word].astype(jnp.int32) for word in range(3))
+        low = low + 32768
+        got_model[group] = ((first << 8) + (low >> 8)).astype(F32) * (1.0 / MODEL_STEPS)
+        got_noise[group] = ((second << 8) + (low & 255)).astype(F32) * (1.0 / NOISE_STEPS)
+        return carry
+
+    lax.fori_loop(0, MEMBERS // BLOCKS, decode, 0)
 
     slots = lax.broadcasted_iota(jnp.int32, (1, CELLS), 1)
     for block in range(BLOCKS):
@@ -342,8 +347,7 @@
 
     for chunk in range(CHUNKS):
         landed(chunk).wait()
-    wait_all(send_sems, 0, got_model.at[others])
-    wait_all(send_sems, 1, got_noise.at[others])
+    wait_all(send_sems, 0, got_coded.at[others])
     one = increment.at[others, pl.ds(0, CHUNK)]
     for chunk in range(CHUNKS):
         wait_all(send_sems, 2 + chunk, one)
@@ -364,6 +368,10 @@
         in_specs=[pl.BlockSpec(memory_space=anywhere)] * 8,
         out_specs=pl.BlockSpec(memory_space=vmem),
         scratch_shapes=[
+            vmem((MEMBERS * BLOCKS, CELLS), F32),
+            vmem((MEMBERS * BLOCKS, CELLS), F32),
+            vmem((MEMBERS, 3, BLOCKS, CELLS), jnp.int16),
+            vmem((MEMBERS, 3, BLOCKS, CELLS), jnp.int16),
             vmem(tile, F32),
             vmem(tile, F32),
             vmem(state, BF16),
@@ -382,10 +390,9 @@
             vmem(state, BF16),
             dma((2 + 2 * CHUNKS,)),
             dma((2 + 2 * CHUNKS,)),
-            dma((8 + CHUNKS,)),
+            dma((9 + CHUNKS,)),
             dma((2, 2)),
             dma((2, 2)),
-            pltpu.SemaphoreType.REGULAR((SIDE,)),
         ],
         compiler_params=pltpu.CompilerParams(collective_id=0, has_side_effects=True),
     )(prior, model, noise, sensor, power, tally, start, listing.T)

time: 79 us -> 76.1 us (0.963)
  Pallas kernels: 77.9 us -> 75 us
    pallas_call x1, Pallas kernels: 77.9 us -> 75 us  [local(): pl.pallas_call(kernel, name='analysis', out_shape=vmem(prior.shape, BF16)...]
where the time goes in v3:
time: 76.1 us; the launch traced here: 75.9 us
  Pallas kernels  75 us (99%)
  local copies, waits for them, and re-layouts  0.97 us (1%)
    pallas_call x1, Pallas kernels, local(): pl.pallas_call(kernel, name='analysis', out_shape=vmem(prior.shape, BF16)...  75 us

profile of v3, /device:TPU:1, one launch (start us, length us, event | category | flops | bytes accessed | tf_op | source)
XLA Modules:
  0.0 75.9 jit_solution(16960171013571145768)
XLA Ops:
  0.0 75.0 %analysis.1 = bf16[1,512,8,128]{3,2,1,0:T(8,128)(2,1)S(1)} custom-call(bf16[1,512,8,128]{3,2,1,0:T(8,128)(2,1)} %prior.1, f32[1,512,128]{2,1,0:T(8,128)} %model.1, f32[1,512,128]{2,1,0:T(8,128)} %noise.1, f32[512,128]{1,0:T(8,128)} %sensor.1, f32[512,128]{1,0:T(8,128)} %power.1, s32[512]{0:T(512)} %tally_hbm.1, s32[4096]{0:T(1024)} %start_hbm.1, ...), custom_call_target="tpu_custom_call" | custom-call | tf_op jit(solution)/shard_map/analysis/pallas_call | solution.py:364
  75.0 1.0 %copy.10 = bf16[1,512,8,128]{3,2,1,0:T(8,128)(2,1)} copy(bf16[1,512,8,128]{3,2,1,0:T(8,128)(2,1)S(1)} %analysis.1) | data formatting | bytes 2097152

commit v4 on v3

--- a/solution.py
+++ b/solution.py
@@ -18,6 +18,7 @@
 BEFORE = 3
 MODEL_STEPS = float(1 << 20)
 NOISE_STEPS = float(1 << 19)
+LINE_STEPS = float((1 << 19) - 1)
 F32 = jnp.float32
 BF16 = jnp.bfloat16
 
@@ -62,7 +63,10 @@
     pattern,
     products,
     partial,
-    got_partial,
+    line_out,
+    line_in,
+    line_unit,
+    got_unit,
     mixing,
     wide_in,
     wide_out,
@@ -271,31 +275,52 @@
 
         lax.fori_loop(0, BLOCKS // 2, body, 0)
 
-    def line_copy(tile, slot, peer):
-        return pltpu.make_async_remote_copy(
-            src_ref=partial.at[tile],
-            dst_ref=got_partial.at[slot],
-            send_sem=line_sems.at[0, slot],
-            recv_sem=line_sems.at[1, slot],
-            device_id=(peer, strip),
-            device_id_type=MESH,
-        )
-
-    fill(0)
-    down = line_copy(0, 0, south)
-    down.start()
-    fill(2)
-    up = line_copy(2, 1, north)
-    up.start()
+    def send_line(tile, slot, peer):
+        fill(tile)
+        pairs = [partial[tile, pair] for pair in range(BLOCKS // 2)]
+        top = jnp.abs(pairs[0])
+        for pair in pairs[1:]:
+            top = jnp.maximum(top, jnp.abs(pair))
+        top = jnp.max(jnp.max(top, axis=0, keepdims=True), axis=1, keepdims=True)
+        top = jnp.maximum(top, 1e-30)
+        factor = LINE_STEPS / top
+        low_bits = jnp.full((MEMBERS, CELLS), -32768, jnp.int32)
+        for at, pair in enumerate(pairs):
+            code = jnp.floor(pair * factor + 0.5).astype(jnp.int32)
+            line_out[slot, at] = (code >> 4).astype(jnp.int16)
+            low_bits = low_bits + ((code & 15) << (4 * at))
+        line_out[slot, BLOCKS // 2] = low_bits.astype(jnp.int16)
+        line_unit[slot] = jnp.broadcast_to(top * (1.0 / LINE_STEPS), (BLOCKS, CELLS))
+        both = [
+            pltpu.make_async_remote_copy(
+                src_ref=src.at[slot],
+                dst_ref=dst.at[slot],
+                send_sem=line_sems.at[0, at],
+                recv_sem=line_sems.at[1, at],
+                device_id=(peer, strip),
+                device_id_type=MESH,
+            )
+            for at, src, dst in ((slot, line_out, line_in), (slot + 2, line_unit, got_unit))
+        ]
+        for copy in both:
+            copy.start()
+        return both
+
+    sent = send_line(0, 0, south) + send_line(2, 1, north)
     for peer in peers:
         for chunk in range(BEFORE, CHUNKS):
             push_prior(chunk, peer)
     fill(1)
-    down.wait()
-    up.wait()
+    for copy in sent:
+        copy.wait()
+
+    def line_part(slot, pair):
+        shared = line_in[slot, BLOCKS // 2].astype(jnp.int32) + 32768
+        code = (line_in[slot, pair].astype(jnp.int32) << 4) + ((shared >> (4 * pair)) & 15)
+        return code.astype(F32) * got_unit[slot, 0:1, :]
 
     for pair in range(BLOCKS // 2):
-        both = partial[1, pair] + got_partial[0, pair] + got_partial[1, pair]
+        both = partial[1, pair] + line_part(0, pair) + line_part(1, pair)
         for item in range(2):
             one = both if item == 0 else pltpu.roll(both, MEMBERS, 1)
             one = one[:, 0:MEMBERS]
@@ -383,7 +408,10 @@
             vmem((3 * BLOCKS, 3 * BLOCKS // 2, CELLS), F32),
             vmem((3, *packed), F32),
             vmem((3, *packed), F32),
-            vmem((2, *packed), F32),
+            vmem((2, BLOCKS // 2 + 1, MEMBERS, CELLS), jnp.int16),
+            vmem((2, BLOCKS // 2 + 1, MEMBERS, CELLS), jnp.int16),
+            vmem((2, BLOCKS, CELLS), F32),
+            vmem((2, BLOCKS, CELLS), F32),
             vmem((BLOCKS, 3, MEMBERS, MEMBERS), BF16),
             vmem((MEMBERS * LEVELS, CELLS), F32),
             vmem((MEMBERS * LEVELS, CELLS), F32),
@@ -392,7 +420,7 @@
             dma((2 + 2 * CHUNKS,)),
             dma((9 + CHUNKS,)),
             dma((2, 2)),
-            dma((2, 2)),
+            dma((2, 4)),
         ],
         compiler_params=pltpu.CompilerParams(collective_id=0, has_side_effects=True),
     )(prior, model, noise, sensor, power, tally, start, listing.T)

time: 76.1 us -> 74.8 us (0.983)
  Pallas kernels: 75 us -> 73.5 us
    pallas_call x1, Pallas kernels: 75 us -> 73.5 us  [local(): pl.pallas_call(kernel, name='analysis', out_shape=vmem(prior.shape, BF16)...]
where the time goes in v4:
time: 74.8 us; the launch traced here: 74.5 us
  Pallas kernels  73.5 us (98%)
  local copies, waits for them, and re-layouts  0.97 us (1%)
    pallas_call x1, Pallas kernels, local(): pl.pallas_call(kernel, name='analysis', out_shape=vmem(prior.shape, BF16)...  73.5 us

profile of v4, /device:TPU:1, one launch (start us, length us, event | category | flops | bytes accessed | tf_op | source)
XLA Modules:
  0.0 74.5 jit_solution(18114405543479429699)
XLA Ops:
  0.0 73.5 %analysis.1 = bf16[1,512,8,128]{3,2,1,0:T(8,128)(2,1)S(1)} custom-call(bf16[1,512,8,128]{3,2,1,0:T(8,128)(2,1)} %prior.1, f32[1,512,128]{2,1,0:T(8,128)} %model.1, f32[1,512,128]{2,1,0:T(8,128)} %noise.1, f32[512,128]{1,0:T(8,128)} %sensor.1, f32[512,128]{1,0:T(8,128)} %power.1, s32[512]{0:T(512)} %tally_hbm.1, s32[4096]{0:T(1024)} %start_hbm.1, ...), custom_call_target="tpu_custom_call" | custom-call | tf_op jit(solution)/shard_map/analysis/pallas_call | solution.py:389
  73.5 1.0 %copy.10 = bf16[1,512,8,128]{3,2,1,0:T(8,128)(2,1)} copy(bf16[1,512,8,128]{3,2,1,0:T(8,128)(2,1)S(1)} %analysis.1) | data formatting | bytes 2097152
